TPU v7x, 512 devices: a whole 4x8x8 slice. The times are simulated.
512 devices in a mesh: ep: 16 (over y, core), tp: 32 (over z, x).
Axes of the slice: x: 4, y: 8, z: 8, core: 2. Of those that a mesh axis runs over, the one named last changes fastest.
Arguments:
- attn_out: bfloat16 [2048, 2048], P('ep'), may hold values from -6 to 6
- residual_in: bfloat16 [2048, 2048], P('ep'), may hold values from -6 to 6
- w_out: bfloat16 [2048, 2048], P(None, 'tp'), may hold values from -0.125 to 0.125
- gain_in: float32 [2048], replicated, may hold values from 0.1 to 1.9
- router_logits: float32 [2048, 8], P('ep'), may hold values from -8 to 8
- expert_ids: int32 [2048, 2], P('ep'), may hold values from 0 to 7, all different within a row; in each aligned block of 128 rows (0 to 127, 128 to 255, ...) at most 64 rows name the same one
- copy_of: int32 [16, 8], replicated, may hold values from 0 to 15, as said below
- w_gate: bfloat16 [16, 2048, 5632], P('ep', None, 'tp')
- w_up: bfloat16 [16, 2048, 5632], P('ep', None, 'tp')
- w_down: bfloat16 [16, 5632, 2048], P('ep', 'tp')
- gain_out: float32 [2048], replicated, may hold values from 0.1 to 1.9
Outputs:
- layer_out: bfloat16 [2048, 2048], P(('ep', 'tp'))
- next_input: bfloat16 [2048, 2048], P(('ep', 'tp'))
Inputs may be any that keep to these rules, and one draw needn't show every extreme that they name: `expert_ids`: each row names 2 different experts. Within the rows of one ep group (aligned blocks of 128 rows) no expert is named by more than 64 rows, and in every draw some group has an expert named by exactly 64 rows. copy_of[s, e] is a copy of expert e, so different experts of one group go to different copies; copies of one expert carry equal weights.
All inputs are finite; a program needn't handle non-finite values.
Results may differ from a plain program's by a relative error of at most 0.019.
Values may be sent and summed in bfloat16 or wider, within the bound.
A program may use at most 64 MiB of HBM per device.

v0:
```python
import jax
import jax.numpy as jnp
from jax import lax
from jax.sharding import PartitionSpec as P


def rms_scale(values, gain):
    mean_square = jnp.mean(values * values, axis=-1, keepdims=True)
    return values * lax.rsqrt(mean_square + 1e-06) * gain


def expert_terms(slots, gate_weight, up_weight, down_weight):
    gate_value = jnp.einsum(
        "scmd,cdf->scmf", slots, gate_weight, preferred_element_type=jnp.float32
    )
    up_value = jnp.einsum("scmd,cdf->scmf", slots, up_weight, preferred_element_type=jnp.float32)
    hidden = (jax.nn.silu(gate_value) * up_value).astype(jnp.bfloat16)
    return jnp.einsum("scmf,cfd->scmd", hidden, down_weight, preferred_element_type=jnp.float32)


def per_device(
    attn_out,
    residual_in,
    w_out,
    gain_in,
    router_logits,
    expert_ids,
    copy_of,
    w_gate,
    w_up,
    w_down,
    gain_out,
):
    group_rows = attn_out.shape[0]
    model_width = attn_out.shape[1]
    tp_count = lax.axis_size("tp")
    ep_count = lax.axis_size("ep")
    own_rows = group_rows // tp_count
    capacity = group_rows // 2
    copies_here = w_gate.shape[0]
    copies_all = copies_here * ep_count
    experts_all = router_logits.shape[1]
    group_index = lax.axis_index("ep")
    tp_index = lax.axis_index("tp")
    columns = jnp.dot(attn_out, w_out, preferred_element_type=jnp.float32).astype(jnp.bfloat16)
    projected = lax.all_gather(columns, "tp", axis=1, tiled=True)
    carried = (residual_in.astype(jnp.float32) + projected.astype(jnp.float32)).astype(jnp.bfloat16)
    normed = rms_scale(carried.astype(jnp.float32), gain_in).astype(jnp.bfloat16)
    expert_grid = jnp.arange(experts_all, dtype=jnp.int32)
    picked = expert_ids[:, :, None] == expert_grid[None, None, :]
    chosen = jnp.sum(jnp.where(picked, router_logits[:, None, :], 0.0), axis=2)
    gate_share = jax.nn.sigmoid(chosen - chosen[:, ::-1])
    group_copies = lax.dynamic_slice_in_dim(copy_of, group_index, 1, 0)[0]
    target = jnp.sum(jnp.where(picked, group_copies[None, None, :], 0), axis=2)
    copy_hits = (
        target[:, :, None] == jnp.arange(copies_all, dtype=jnp.int32)[None, None, :]
    ).astype(jnp.int32)
    per_row = jnp.sum(copy_hits, axis=1)
    before = jnp.cumsum(per_row, axis=0) - per_row
    position = jnp.sum(copy_hits * before[:, None, :], axis=2)
    slot_index = target * capacity + position
    row_numbers = jnp.broadcast_to(
        jnp.arange(group_rows, dtype=jnp.int32)[:, None], slot_index.shape
    )
    slot_rows = (
        jnp.zeros((copies_all * capacity,), jnp.int32)
        .at[slot_index.reshape(-1)]
        .set(row_numbers.reshape(-1))
    )
    rows_table = slot_rows.reshape(ep_count, copies_here, capacity)
    outgoing = jnp.take(normed, rows_table, axis=0)
    arrived = lax.all_to_all(outgoing, "ep", split_axis=0, concat_axis=0, tiled=True)
    partial_value = expert_terms(arrived, w_gate, w_up, w_down)
    summed = lax.psum_scatter(
        partial_value.astype(jnp.bfloat16), "tp", scatter_dimension=2, tiled=True
    )
    returned = lax.all_to_all(summed, "ep", split_axis=0, concat_axis=0, tiled=True)
    own_target = lax.dynamic_slice_in_dim(target, tp_index * own_rows, own_rows, 0)
    own_position = lax.dynamic_slice_in_dim(position, tp_index * own_rows, own_rows, 0)
    own_gates = lax.dynamic_slice_in_dim(gate_share, tp_index * own_rows, own_rows, 0)
    portion = lax.all_gather(returned, "tp", axis=2, tiled=True)
    span_rows = portion.shape[2]
    flat_portion = portion.reshape(copies_all, span_rows, model_width)
    inside = (own_position >= 0) & (own_position < span_rows)
    picked_rows = flat_portion[own_target, jnp.clip(own_position, 0, span_rows - 1)]
    row_weights = jnp.where(inside, own_gates, 0.0)
    mixture = jnp.sum(row_weights[:, :, None] * picked_rows.astype(jnp.float32), axis=1)
    own_carried = lax.dynamic_slice_in_dim(carried, tp_index * own_rows, own_rows, 0)
    layer_out = (own_carried.astype(jnp.float32) + mixture).astype(jnp.bfloat16)
    next_input = rms_scale(layer_out.astype(jnp.float32), gain_out).astype(jnp.bfloat16)
    return (layer_out, next_input)


def solution(mesh):
    return jax.shard_map(
        per_device,
        mesh=mesh,
        in_specs=(
            P("ep", None),
            P("ep", None),
            P(None, "tp"),
            P(),
            P("ep", None),
            P("ep", None),
            P(),
            P("ep", None, "tp"),
            P("ep", None, "tp"),
            P("ep", "tp", None),
            P(),
        ),
        out_specs=(P(("ep", "tp"), None), P(("ep", "tp"), None)),
        check_vma=False,
    )
```

profile of v0, /device:TPU:8, one launch (start us, length us, event | category | flops | bytes accessed | tf_op | source)
XLA Modules:
  0.0 536.4 jit_solution(7059032426642041962)
XLA Ops:
  7.2 0.0 copy-start
  7.2 0.0 copy-start.3
  7.2 0.0 reduce-scatter.2.cloned.1.call-start
  7.2 0.9 dynamic-slice_reduce_fusion
  8.2 0.8 select_reduce_fusion.2
  8.9 0.1 copy.68
  9.0 0.2 reduce_window_sum.11
  9.2 0.1 copy.70
  9.3 0.1 copy.72
  9.4 0.1 add.110
  9.6 0.1 reshape.207
  9.8 1.4 scatter_custom_fusion
  11.2 0.1 reshape.182
  11.2 0.1 reshape.181
  11.3 0.1 reshape.191
  11.4 1.4 convolution_convert_fusion
  12.8 55.7 %all_gather.6 = bf16[128,2048]{0,1:T(8,128)(2,1)S(1)} all-gather(bf16[128,64]{0,1:T(8,128)(2,1)S(1)} %convolution_convert_fusion), channel_id=1, replica_groups=mesh['ep'=16,'tp'=32] {'tp'}, dimensions={1}, use_global_device_ids=true | all-gather | bytes 540672 | tf_op jit(solution)/shard_map/all_gather | solution.py:46
  68.5 0.2 copy.67
  68.7 1.3 fusion.19
  70.0 0.0 copy-done.3
  70.0 0.2 fusion.21
  70.2 6.0 %gather_fusion = bf16[1024,2048]{1,0:T(8,128)(2,1)} fusion(bf16[128,2048]{1,0:T(8,128)(2,1)S(1)} %fusion.21, s32[1024]{0:T(1024)S(1)} %broadcast_clamp_fusion), kind=kCustom, calls=%fused_computation | custom fusion | bytes 8392704 | tf_op jit(solution)/shard_map/jit(_take)/gather | solution.py:71
  76.3 2.6 broadcast_select_fusion
  78.9 0.0 copy-start.7
  78.9 100.5 %all_to_all.10 = bf16[16,1,64,2048]{3,2,1,0:T(8,128)(2,1)S(1)} all-to-all(bf16[16,1,64,2048]{3,2,1,0:T(8,128)(2,1)S(1)} %broadcast_select_fusion), channel_id=1, replica_groups=mesh['ep'=16,'tp'=32] {'ep'}, dimensions={0} | all-to-all | bytes 8388608 | tf_op jit(solution)/shard_map/all_to_all | solution.py:72
  179.4 0.0 copy-start.1
  179.4 2.0 copy-done.1
  181.4 0.0 copy-done.7
  181.4 0.0 copy-start.8
  181.4 2.3 fusion.4
  183.7 0.0 copy-done
  183.7 0.0 copy-done.8
  183.7 8.8 %convert_bitcast_fusion = bf16[16,1,64,2048]{3,2,0,1:T(8,128)(2,1)} fusion(bf16[16,1,64,2048]{3,2,1,0:T(8,128)(2,1)} %copy-done.1, f32[16,1,64,176]{3,2,0,1:T(8,128)} %fusion.4, bf16[1,176,2048]{2,1,0:T(8,128)(2,1)S(1)} %copy-done, bf16[1,2048,176]{1,2,0:T(8,128)(2,1)S(1)} %copy-done.8), kind=kOutput, calls=%fused_computation.8 | convolution fusion | flops 1479573504 | bytes 10551296 | tf_op jit(solution)/shard_map/scmf,cfd->scmd/dot_general | solution.py:18
  192.5 6.5 %copy.74 = bf16[16,1,64,2048]{3,0,1,2:T(8,128)(2,1)} copy(bf16[16,1,64,2048]{3,2,0,1:T(8,128)(2,1)} %convert_bitcast_fusion) | data formatting | bytes 8388608 | tf_op jit(solution)/shard_map/convert_element_type | solution.py:75
  198.9 0.0 copy-start.5
  198.9 0.0 copy-start.6
  198.9 0.0 reduce-scatter.2.cloned.1.call-update
  199.0 0.0 all-gather.2.cloned.1.call-start
  199.0 221.9 %reduce-scatter.2.cloned.1.call-done = bf16[16,1,2,2048]{3,0,1,2:T(8,128)(2,1)} async-done(((bf16[16,1,64,2048]{3,0,1,2:T(8,128)(2,1)}), bf16[16,1,2,2048]{3,0,1,2:T(8,128)(2,1)}) %reduce-scatter.2.cloned.1.call-update) | async-done | bytes 131088 | tf_op jit(solution)/shard_map/reduce_scatter | solution.py:74
  420.9 1.0 copy.75
  422.0 14.5 %all_to_all.11 = bf16[16,1,2,2048]{3,2,1,0:T(2,128)(2,1)S(1)} all-to-all(bf16[16,1,2,2048]{3,2,1,0:T(2,128)(2,1)S(1)} %copy.75), channel_id=1, replica_groups=mesh['ep'=16,'tp'=32] {'ep'}, dimensions={0} | all-to-all | bytes 262144 | tf_op jit(solution)/shard_map/all_to_all | solution.py:77
  436.5 0.7 copy.76
  437.2 0.0 all-gather.2.cloned.1.call-update
  437.2 0.1 fusion.37
  437.3 0.1 copy.78
  437.4 0.1 reshape.197
  437.5 0.0 copy-done.5
  437.5 0.0 copy-done.6
  437.6 0.1 and_select_fusion
  437.6 0.1 copy.71
  437.7 0.0 copy-start.4
  437.7 82.9 %all-gather.2.cloned.1.call-done = bf16[16,1,64,2048]{3,0,1,2:T(8,128)(2,1)} async-done(((bf16[16,1,2,2048]{3,0,1,2:T(8,128)(2,1)}), bf16[16,1,64,2048]{3,0,1,2:T(8,128)(2,1)}) %all-gather.2.cloned.1.call-update) | async-done | bytes 4194320 | tf_op jit(solution)/shard_map/all_gather | solution.py:81
  520.6 6.5 %copy.80 = bf16[16,1,64,2048]{3,2,0,1:T(8,128)(2,1)} copy(bf16[16,1,64,2048]{3,0,1,2:T(8,128)(2,1)} %all-gather.2.cloned.1.call-done) | data formatting | bytes 8388608 | tf_op jit(solution)/shard_map/all_gather | solution.py:81
  527.0 1.4 gather_fusion.1
  528.5 0.2 multiply_reduce_fusion
  528.7 0.1 fusion.29
  528.8 0.0 copy-start.2
  528.8 0.0 copy-done.4
  528.8 0.7 fusion.31
  529.5 0.0 copy-done.2
  (15 shorter events, 0.2 us)
Async XLA Ops:
  7.2 176.5 %copy-start = (bf16[1,176,2048]{2,1,0:T(8,128)(2,1)S(1)}, bf16[1,176,2048]{2,1,0:T(8,128)(2,1)}, u32[]{:S(2)}) copy-start(bf16[1,176,2048]{2,1,0:T(8,128)(2,1)} %param.20) | copy-start | bytes 2162692
  7.2 62.8 %copy-start.3 = (f32[2048]{0:T(1024)S(1)}, f32[2048]{0:T(1024)}, u32[]{:S(2)}) copy-start(f32[2048]{0:T(1024)} %param.14) | copy-start | bytes 24580
  7.2 413.7 %reduce-scatter.2.cloned.1.call-start = ((), (), s32[]{:S(2)}) async-start(), calls=%async_computation.3 | async-start | bytes 4325376 | tf_op jit(solution)/shard_map/reduce_scatter | solution.py:74
  78.9 102.5 %copy-start.7 = (bf16[1,2048,176]{1,2,0:T(8,128)(2,1)S(1)}, bf16[1,2048,176]{1,2,0:T(8,128)(2,1)}, u32[]{:S(2)}) copy-start(bf16[1,2048,176]{1,2,0:T(8,128)(2,1)} %param.18) | copy-start | bytes 2162692
  179.4 2.0 copy-start.1
  181.4 2.3 copy-start.8
  198.9 238.6 %copy-start.5 = (f32[128,8]{0,1:T(8,128)S(1)}, f32[128,8]{0,1:T(8,128)}, u32[]{:S(2)}) copy-start(f32[128,8]{0,1:T(8,128)} %param.15) | copy-start | bytes 12292
  198.9 238.6 %copy-start.6 = (s32[128,2]{0,1:T(2,128)S(1)}, s32[128,2]{0,1:T(2,128)}, u32[]{:S(2)}) copy-start(s32[128,2]{0,1:T(2,128)} %param.16) | copy-start | bytes 3076
  199.0 321.6 %all-gather.2.cloned.1.call-start = ((), (), s32[]{:S(2)}) async-start(), calls=%async_computation.4 | async-start | bytes 4325376 | tf_op jit(solution)/shard_map/all_gather | solution.py:81
  437.7 91.1 %copy-start.4 = (f32[2048]{0:T(1024)S(1)}, f32[2048]{0:T(1024)}, u32[]{:S(2)}) copy-start(f32[2048]{0:T(1024)} %param.21) | copy-start | bytes 24580
  528.8 0.7 copy-start.2
Sparse Core Ops, SparseCore 0:
  199.1 221.8 reduce-scatter.1
  437.3 83.1 all-gather.1
where the time goes:
time: 537 us; the launch traced here: 536 us
  waiting for transfers between devices  305 us (57%)
  blocking collectives  171 us (32%)
  local copies, waits for them, and re-layouts  27.7 us (5%)
  between operations  14.2 us (3%)
  matrix products  12.5 us (2%)
  other arithmetic  6.33 us (1%)
    reduce_scatter x1, waiting for transfers between devices, per_device(): lax.psum_scatter(partial_value.astype(jnp.bfloat16), 'tp', scatter_dimens...  222 us
    all_to_all x1, blocking collectives, per_device(): lax.all_to_all(outgoing, 'ep', split_axis=0, concat_axis=0, tiled=True)  100 us
    all_gather x1, waiting for transfers between devices, per_device(): portion = lax.all_gather(returned, 'tp', axis=2, tiled=True)  82.9 us
    all_gather x1, blocking collectives, per_device(): projected = lax.all_gather(columns, 'tp', axis=1, tiled=True)  55.7 us
    all_to_all x1, blocking collectives, per_device(): lax.all_to_all(summed, 'ep', split_axis=0, concat_axis=0, tiled=True)  14.5 us
  transfers between devices with their start and end apart: 2, of which 2 were waited for; matrix products, arithmetic and copies ran while one was open for 0% of the time, Pallas kernels for 0%

commit v1 on v0

--- a/solution.py
+++ b/solution.py
@@ -43,7 +43,9 @@
     group_index = lax.axis_index("ep")
     tp_index = lax.axis_index("tp")
     columns = jnp.dot(attn_out, w_out, preferred_element_type=jnp.float32).astype(jnp.bfloat16)
-    projected = lax.all_gather(columns, "tp", axis=1, tiled=True)
+    projected = jnp.concatenate(
+        lax.all_to_all(jnp.stack([columns] * lax.axis_size("tp")), "tp", 0, 0), axis=1
+    )
     carried = (residual_in.astype(jnp.float32) + projected.astype(jnp.float32)).astype(jnp.bfloat16)
     normed = rms_scale(carried.astype(jnp.float32), gain_in).astype(jnp.bfloat16)
     expert_grid = jnp.arange(experts_all, dtype=jnp.int32)

time: 537 us -> 508 us (0.946)
  blocking collectives: 171 us -> 115 us
  starting transfers between devices: 0.08 us -> 13.2 us
  waiting for transfers between devices: 305 us -> 318 us
    all_gather x1 -> x0, blocking collectives: 55.7 us -> none  [per_device(): projected = lax.all_gather(columns, 'tp', axis=1, tiled=True)]
    all_to_all x0 -> x1, waiting for transfers between devices: none -> 13.5 us  [per_device(): lax.all_to_all(jnp.stack([columns] * lax.axis_size('tp')), 'tp', 0, 0)]
    all_to_all x0 -> x1, starting transfers between devices: none -> 13.2 us  [per_device(): lax.all_to_all(jnp.stack([columns] * lax.axis_size('tp')), 'tp', 0, 0)]
  transfers between devices with their start and end apart: 2 -> 3, of which waited for: 2 -> 3; matrix products, arithmetic and copies ran while one was open for 0% -> 1% of each run, Pallas kernels for 0% -> 0%
where the time goes in v1:
time: 508 us; the launch traced here: 507 us
  waiting for transfers between devices  318 us (63%)
  blocking collectives  115 us (23%)
  local copies, waits for them, and re-layouts  28.7 us (6%)
  between operations  14.2 us (3%)
  starting transfers between devices  13.2 us (3%)
  matrix products  12.6 us (2%)
  other arithmetic  5.36 us (1%)
    reduce_scatter x1, waiting for transfers between devices, per_device(): lax.psum_scatter(partial_value.astype(jnp.bfloat16), 'tp', scatter_dimens...  222 us
    all_to_all x1, blocking collectives, per_device(): lax.all_to_all(outgoing, 'ep', split_axis=0, concat_axis=0, tiled=True)  100 us
    all_gather x1, waiting for transfers between devices, per_device(): portion = lax.all_gather(returned, 'tp', axis=2, tiled=True)  83 us
    all_to_all x1, blocking collectives, per_device(): lax.all_to_all(summed, 'ep', split_axis=0, concat_axis=0, tiled=True)  14.5 us
    all_to_all x1, waiting for transfers between devices, per_device(): lax.all_to_all(jnp.stack([columns] * lax.axis_size('tp')), 'tp', 0, 0)  13.5 us
    all_to_all x1, starting transfers between devices, per_device(): lax.all_to_all(jnp.stack([columns] * lax.axis_size('tp')), 'tp', 0, 0)  13.2 us
  transfers between devices with their start and end apart: 3, of which 3 were waited for; matrix products, arithmetic and copies ran while one was open for 1% of the time, Pallas kernels for 0%

profile of v1, /device:TPU:8, one launch (start us, length us, event | category | flops | bytes accessed | tf_op | source)
XLA Modules:
  0.0 507.4 jit_solution(17217444996815037729)
XLA Ops:
  7.2 0.0 copy-start
  7.2 0.0 copy-start.2
  7.2 1.5 convolution_convert_fusion
  8.7 0.0 copy-start.4
  8.7 0.9 stack.2
  9.6 13.2 %all-to-all-start = ((bf16[32,128,64]{1,2,0:T(8,128)(2,1)}), bf16[32,128,64]{1,2,0:T(8,128)(2,1)S(1)}, u32[]{:S(2)}, u32[]{:S(2)}) async-start(bf16[32,128,64]{1,2,0:T(8,128)(2,1)} %stack.2), calls=%async_computation | async-start | bytes 1048576 | tf_op jit(solution)/shard_map/all_to_all | solution.py:47
  22.8 0.0 reduce-scatter.2.cloned.1.call-start
  22.8 0.9 dynamic-slice_reduce_fusion
  23.7 0.8 select_reduce_fusion.2
  24.5 0.1 copy.28
  24.6 0.2 reduce_window_sum.11
  24.8 0.1 copy.30
  24.9 0.1 copy.32
  25.0 0.1 add.110
  25.2 0.1 reshape.214
  25.3 1.4 scatter_custom_fusion
  26.7 0.1 reshape.188
  26.8 0.1 reshape.187
  26.9 0.1 reshape.198
  27.0 13.5 %all-to-all-done = bf16[32,128,64]{1,2,0:T(8,128)(2,1)S(1)} async-done(((bf16[32,128,64]{1,2,0:T(8,128)(2,1)}), bf16[32,128,64]{1,2,0:T(8,128)(2,1)S(1)}, u32[]{:S(2)}, u32[]{:S(2)}) %all-to-all-start) | async-done | bytes 524320 | tf_op jit(solution)/shard_map/all_to_all | solution.py:47
  40.5 0.1 convert_element_type.77
  40.6 0.3 copy.27
  41.0 0.0 copy-done.2
  41.0 0.2 fusion.19
  41.2 0.0 copy-done.4
  41.2 0.2 fusion.21
  41.4 6.0 %gather_fusion = bf16[1024,2048]{1,0:T(8,128)(2,1)} fusion(bf16[128,2048]{1,0:T(8,128)(2,1)S(1)} %fusion.21, s32[1024]{0:T(1024)S(1)} %broadcast_clamp_fusion), kind=kCustom, calls=%fused_computation | custom fusion | bytes 8392704 | tf_op jit(solution)/shard_map/jit(_take)/gather | solution.py:73
  47.4 2.6 broadcast_select_fusion
  50.1 0.0 copy-start.8
  50.1 100.5 %all_to_all.15 = bf16[16,1,64,2048]{3,2,1,0:T(8,128)(2,1)S(1)} all-to-all(bf16[16,1,64,2048]{3,2,1,0:T(8,128)(2,1)S(1)} %broadcast_select_fusion), channel_id=1, replica_groups=mesh['ep'=16,'tp'=32] {'ep'}, dimensions={0} | all-to-all | bytes 8388608 | tf_op jit(solution)/shard_map/all_to_all | solution.py:74
  150.6 0.0 copy-start.1
  150.6 2.0 copy-done.1
  152.6 0.0 copy-done.8
  152.6 0.0 copy-start.9
  152.6 2.3 fusion.4
  154.9 0.0 copy-done
  154.9 0.0 copy-done.9
  154.9 8.8 %convert_bitcast_fusion = bf16[16,1,64,2048]{3,2,0,1:T(8,128)(2,1)} fusion(bf16[16,1,64,2048]{3,2,1,0:T(8,128)(2,1)} %copy-done.1, f32[16,1,64,176]{3,2,0,1:T(8,128)} %fusion.4, bf16[1,176,2048]{2,1,0:T(8,128)(2,1)S(1)} %copy-done, bf16[1,2048,176]{1,2,0:T(8,128)(2,1)S(1)} %copy-done.9), kind=kOutput, calls=%fused_computation.8 | convolution fusion | flops 1479573504 | bytes 10551296 | tf_op jit(solution)/shard_map/scmf,cfd->scmd/dot_general | solution.py:18
  163.7 6.5 %copy.34 = bf16[16,1,64,2048]{3,0,1,2:T(8,128)(2,1)} copy(bf16[16,1,64,2048]{3,2,0,1:T(8,128)(2,1)} %convert_bitcast_fusion) | data formatting | bytes 8388608 | tf_op jit(solution)/shard_map/convert_element_type | solution.py:77
  170.1 0.0 copy-start.6
  170.1 0.0 copy-start.7
  170.1 0.0 reduce-scatter.2.cloned.1.call-update
  170.2 0.0 all-gather.2.cloned.1.call-start
  170.2 221.6 %reduce-scatter.2.cloned.1.call-done = bf16[16,1,2,2048]{3,0,1,2:T(8,128)(2,1)} async-done(((bf16[16,1,64,2048]{3,0,1,2:T(8,128)(2,1)}), bf16[16,1,2,2048]{3,0,1,2:T(8,128)(2,1)}) %reduce-scatter.2.cloned.1.call-update) | async-done | bytes 131088 | tf_op jit(solution)/shard_map/reduce_scatter | solution.py:76
  391.9 1.0 copy.35
  392.9 14.5 %all_to_all.16 = bf16[16,1,2,2048]{3,2,1,0:T(2,128)(2,1)S(1)} all-to-all(bf16[16,1,2,2048]{3,2,1,0:T(2,128)(2,1)S(1)} %copy.35), channel_id=1, replica_groups=mesh['ep'=16,'tp'=32] {'ep'}, dimensions={0} | all-to-all | bytes 262144 | tf_op jit(solution)/shard_map/all_to_all | solution.py:79
  407.4 0.7 copy.36
  408.1 0.0 all-gather.2.cloned.1.call-update
  408.1 0.1 fusion.37
  408.2 0.1 copy.38
  408.3 0.1 reshape.204
  408.3 0.0 copy-done.6
  408.3 0.0 copy-done.7
  408.4 0.1 and_select_fusion
  408.5 0.1 copy.31
  408.6 0.0 copy-start.5
  408.6 83.0 %all-gather.2.cloned.1.call-done = bf16[16,1,64,2048]{3,0,1,2:T(8,128)(2,1)} async-done(((bf16[16,1,2,2048]{3,0,1,2:T(8,128)(2,1)}), bf16[16,1,64,2048]{3,0,1,2:T(8,128)(2,1)}) %all-gather.2.cloned.1.call-update) | async-done | bytes 4194320 | tf_op jit(solution)/shard_map/all_gather | solution.py:83
  491.6 6.5 %copy.40 = bf16[16,1,64,2048]{3,2,0,1:T(8,128)(2,1)} copy(bf16[16,1,64,2048]{3,0,1,2:T(8,128)(2,1)} %all-gather.2.cloned.1.call-done) | data formatting | bytes 8388608 | tf_op jit(solution)/shard_map/all_gather | solution.py:83
  498.0 1.4 gather_fusion.1
  499.5 0.2 multiply_reduce_fusion
  499.7 0.1 fusion.29
  499.8 0.0 copy-done.5
  499.8 0.7 fusion.31
  500.5 0.0 copy-done.3
  (16 shorter events, 0.2 us)
Async XLA Ops:
  7.2 147.7 %copy-start = (bf16[1,176,2048]{2,1,0:T(8,128)(2,1)S(1)}, bf16[1,176,2048]{2,1,0:T(8,128)(2,1)}, u32[]{:S(2)}) copy-start(bf16[1,176,2048]{2,1,0:T(8,128)(2,1)} %param.20) | copy-start | bytes 2162692
  7.2 33.8 %copy-start.2 = (bf16[128,2048]{1,0:T(8,128)(2,1)S(1)}, bf16[128,2048]{1,0:T(8,128)(2,1)}, u32[]{:S(2)}) copy-start(bf16[128,2048]{1,0:T(8,128)(2,1)} %param.12) | copy-start | bytes 1572868
  8.7 32.5 %copy-start.4 = (f32[2048]{0:T(1024)S(1)}, f32[2048]{0:T(1024)}, u32[]{:S(2)}) copy-start(f32[2048]{0:T(1024)} %param.14) | copy-start | bytes 24580
  9.6 30.9 %all-to-all-start = ((bf16[32,128,64]{1,2,0:T(8,128)(2,1)}), bf16[32,128,64]{1,2,0:T(8,128)(2,1)S(1)}, u32[]{:S(2)}, u32[]{:S(2)}) async-start(bf16[32,128,64]{1,2,0:T(8,128)(2,1)} %stack.2), calls=%async_computation | async-start | bytes 1048576 | tf_op jit(solution)/shard_map/all_to_all | solution.py:47
  22.8 369.1 %reduce-scatter.2.cloned.1.call-start = ((), (), s32[]{:S(2)}) async-start(), calls=%async_computation.4 | async-start | bytes 4325376 | tf_op jit(solution)/shard_map/reduce_scatter | solution.py:76
  50.1 102.5 %copy-start.8 = (bf16[1,2048,176]{1,2,0:T(8,128)(2,1)S(1)}, bf16[1,2048,176]{1,2,0:T(8,128)(2,1)}, u32[]{:S(2)}) copy-start(bf16[1,2048,176]{1,2,0:T(8,128)(2,1)} %param.18) | copy-start | bytes 2162692
  150.6 2.0 copy-start.1
  152.6 2.3 copy-start.9
  170.1 238.2 %copy-start.6 = (f32[128,8]{0,1:T(8,128)S(1)}, f32[128,8]{0,1:T(8,128)}, u32[]{:S(2)}) copy-start(f32[128,8]{0,1:T(8,128)} %param.15) | copy-start | bytes 12292
  170.1 238.2 %copy-start.7 = (s32[128,2]{0,1:T(2,128)S(1)}, s32[128,2]{0,1:T(2,128)}, u32[]{:S(2)}) copy-start(s32[128,2]{0,1:T(2,128)} %param.16) | copy-start | bytes 3076
  170.2 321.4 %all-gather.2.cloned.1.call-start = ((), (), s32[]{:S(2)}) async-start(), calls=%async_computation.5 | async-start | bytes 4325376 | tf_op jit(solution)/shard_map/all_gather | solution.py:83
  408.6 91.2 %copy-start.5 = (f32[2048]{0:T(1024)S(1)}, f32[2048]{0:T(1024)}, u32[]{:S(2)}) copy-start(f32[2048]{0:T(1024)} %param.21) | copy-start | bytes 24580
  499.8 0.7 copy-start.3
Sparse Core Ops, SparseCore 0:
  170.3 221.5 reduce-scatter.1
  408.2 83.3 all-gather.1
